TPU v7x, 256 devices: a whole 4x4x8 slice. The times are simulated.
256 devices in a mesh: clip: 16 (over y_lo, z), chan: 16 (over x, y_hi, core).
Axes of the slice: x: 4, y: 4 (y_hi: 2, y_lo: 2; y = y_hi * 2 + y_lo), z: 8, core: 2. Of those that a mesh axis runs over, the one named last changes fastest.
Arguments:
- block_in: bfloat16 [16, 512, 4, 4, 128], P('clip', 'chan'), may hold values from -6 to 6
- conv_one: bfloat16 [512, 27, 512], P('chan'), may hold values from -0.0546875 to 0.0546875
- conv_two: bfloat16 [512, 27, 512], P('chan'), may hold values from -0.0546875 to 0.0546875
- out_cotangent: bfloat16 [16, 512, 4, 4, 128], P('clip', 'chan'), may hold values from -6 to 6
Outputs:
- block_out: float32 [16, 512, 4, 4, 128], P('clip', 'chan')
- block_in_grad: float32 [16, 512, 4, 4, 128], P('clip', 'chan')
- conv_one_grad: float32 [512, 27, 512], P('chan')
- conv_two_grad: float32 [512, 27, 512], P('chan')
All inputs are finite; a program needn't handle non-finite values.
Results may differ from a plain program's by a relative error of at most 0.0046.
Values may be sent and summed in bfloat16 or wider, within the bound.
No kernel may reach another device: no remote copies, remote signals or barrier semaphores. Data moves between devices by JAX's collectives and lax.ppermute only.
A program may use at most 64 MiB of HBM per device.

v0:
```python
import jax
import jax.numpy as jnp
from jax import lax
from jax.sharding import PartitionSpec as P

C = 512
GROUPS = 32


def norm_act(field):
    shape = field.shape
    size = C // GROUPS
    grouped = field.reshape(shape[0] // size, size, -1)
    center = jnp.mean(grouped, axis=(1, 2), keepdims=True)
    spread = jnp.mean((grouped - center) ** 2, axis=(1, 2), keepdims=True)
    normed = (grouped - center) * lax.rsqrt(spread + 1e-06)
    return jax.nn.silu(normed).reshape(shape)


def tap_list():
    return [(t_tap, h_tap, w_tap) for t_tap in range(3) for h_tap in range(3) for w_tap in range(3)]


def forward_shift(field, t_tap, h_tap, w_tap):
    frames, height, width = (field.shape[1], field.shape[2], field.shape[3])
    padded = jnp.pad(field, ((0, 0), (2, 0), (1, 1), (1, 1)))
    return padded[:, t_tap : t_tap + frames, h_tap : h_tap + height, w_tap : w_tap + width]


def backward_shift(field, t_tap, h_tap, w_tap):
    frames, height, width = (field.shape[1], field.shape[2], field.shape[3])
    padded = jnp.pad(field, ((0, 0), (0, 2), (1, 1), (1, 1)))
    return padded[
        :,
        2 - t_tap : 2 - t_tap + frames,
        2 - h_tap : 2 - h_tap + height,
        2 - w_tap : 2 - w_tap + width,
    ]


def conv_gathered(acts_full, kernel):
    products = jnp.einsum("cthw,okc->kothw", acts_full, kernel, preferred_element_type=jnp.float32)
    total = None
    for index, (t_tap, h_tap, w_tap) in enumerate(tap_list()):
        moved = forward_shift(products[index], t_tap, h_tap, w_tap)
        total = moved if total is None else total + moved
    return total


def spread_columns(grads):
    pieces = [backward_shift(grads, t_tap, h_tap, w_tap) for t_tap, h_tap, w_tap in tap_list()]
    return jnp.stack(pieces, axis=0)


def shards(block_in, conv_one, conv_two, out_cotangent):
    in_float = block_in[0].astype(jnp.float32)
    cotangent = out_cotangent[0]
    first_float, first_pull = jax.vjp(norm_act, in_float)
    act_one_local = first_float.astype(jnp.bfloat16)
    act_one = lax.all_gather(act_one_local, "chan", axis=0, tiled=True)
    hidden = conv_gathered(act_one, conv_one)
    second_float, second_pull = jax.vjp(norm_act, hidden)
    act_two_local = second_float.astype(jnp.bfloat16)
    act_two = lax.all_gather(act_two_local, "chan", axis=0, tiled=True)
    block_out = in_float + conv_gathered(act_two, conv_two)
    cot_columns = spread_columns(cotangent)
    two_grad = jnp.einsum(
        "cthw,kothw->okc", act_two, cot_columns, preferred_element_type=jnp.float32
    )
    partial_two = jnp.einsum(
        "kothw,okc->cthw", cot_columns, conv_two, preferred_element_type=jnp.float32
    )
    act_two_grad = lax.psum_scatter(partial_two, "chan", scatter_dimension=0, tiled=True)
    hidden_grad = second_pull(act_two_grad)[0].astype(jnp.bfloat16)
    hidden_columns = spread_columns(hidden_grad)
    one_grad = jnp.einsum(
        "cthw,kothw->okc", act_one, hidden_columns, preferred_element_type=jnp.float32
    )
    partial_one = jnp.einsum(
        "kothw,okc->cthw", hidden_columns, conv_one, preferred_element_type=jnp.float32
    )
    act_one_grad = lax.psum_scatter(partial_one, "chan", scatter_dimension=0, tiled=True)
    in_grad = cotangent.astype(jnp.float32) + first_pull(act_one_grad)[0]
    one_grad, two_grad = lax.psum((one_grad, two_grad), "clip")
    return (block_out[None], in_grad[None], one_grad, two_grad)


def solution(mesh):
    in_specs = (
        P("clip", "chan", None, None, None),
        P("chan", None, None),
        P("chan", None, None),
        P("clip", "chan", None, None, None),
    )
    out_specs = (
        P("clip", "chan", None, None, None),
        P("clip", "chan", None, None, None),
        P("chan", None, None),
        P("chan", None, None),
    )
    return jax.shard_map(shards, mesh=mesh, in_specs=in_specs, out_specs=out_specs, check_vma=False)
```

profile of v0, /device:TPU:2, one launch (start us, length us, event | category | flops | bytes accessed | tf_op | source)
XLA Modules:
  0.0 473.6 jit_solution(7996357429404227542)
XLA Ops:
  7.2 1.1 convert_reduce_fusion
  8.7 1.1 fusion.58
  10.2 1.7 fusion.47
  12.0 0.9 copy.76
  15.3 2.4 fusion.4
  17.8 2.2 copy.75
  20.1 49.3 %all-gather.3.cloned.1.call-done = bf16[512,4,4,128]{3,0,2,1:T(8,128)(2,1)} async-done(((bf16[32,4,4,128]{3,0,2,1:T(8,128)(2,1)}), bf16[512,4,4,128]{3,0,2,1:T(8,128)(2,1)}) %all-gather.3.cloned.1.call-update) | async-done | bytes 2097168 | tf_op jit(solution)/shard_map/all_gather | solution.py:60
  69.3 3.6 convolution_bitcast_fusion.1
  72.9 0.2 slice_bitcast_fusion.52
  73.2 1.0 slice_bitcast_fusion.53
  74.2 0.9 fusion.222
  76.1 84.6 %reduce-scatter.3.cloned.1.call-done = f32[32,4,4,128]{3,0,2,1:T(8,128)} async-done(((f32[512,4,4,128]{3,0,2,1:T(8,128)}), f32[32,4,4,128]{3,0,2,1:T(8,128)}) %reduce-scatter.3.cloned.1.call-update) | async-done | bytes 262160 | tf_op jit(solution)/shard_map/reduce_scatter | solution.py:73
  160.7 1.3 multiply_reduce_fusion.3
  163.2 0.9 add_convert_fusion
  164.0 0.2 reduce-scatter.5.cloned.1.call-start
  166.6 2.4 fusion.7
  169.0 2.2 copy.74
  171.3 5.9 %fusion.16 = f32[32,27,512]{2,0,1:T(8,128)} fusion(bf16[27,32,4,4,128]{4,1,3,2,0:T(8,128)(2,1)} %copy-done.6, bf16[512,4,4,128]{3,0,2,1:T(8,128)(2,1)} %all-gather.3.cloned.1.call-done), kind=kOutput, calls=%fused_computation.68 | convolution fusion | flops 1811939328 | bytes 7405568 | tf_op jit(solution)/shard_map/cthw,kothw->okc/dot_general | solution.py:76
  177.2 40.5 %all-gather.5.cloned.1.call-done = bf16[512,4,4,128]{3,0,2,1:T(8,128)(2,1)} async-done(((bf16[32,4,4,128]{3,0,2,1:T(8,128)(2,1)}), bf16[512,4,4,128]{3,0,2,1:T(8,128)(2,1)}) %all-gather.5.cloned.1.call-update) | async-done | bytes 2097168 | tf_op jit(solution)/shard_map/all_gather | solution.py:64
  217.7 5.9 %fusion.19 = f32[32,27,512]{2,0,1:T(8,128)} fusion(bf16[27,32,4,4,128]{4,1,3,2,0:T(8,128)(2,1)} %copy-done.5, bf16[512,4,4,128]{3,0,2,1:T(8,128)(2,1)} %all-gather.5.cloned.1.call-done), kind=kOutput, calls=%fused_computation.69 | convolution fusion | flops 1811939328 | bytes 7405568 | tf_op jit(solution)/shard_map/cthw,kothw->okc/dot_general | solution.py:67
  223.6 3.6 convolution_bitcast_fusion
  227.4 1.0 slice_bitcast_fusion.26
  228.4 0.8 fusion.55
  229.3 0.9 copy.21
  230.2 78.7 %reduce-scatter.5.cloned.1.call-done = f32[32,4,4,128]{3,0,2,1:T(8,128)} async-done(((f32[512,4,4,128]{3,0,2,1:T(8,128)}), f32[32,4,4,128]{3,0,2,1:T(8,128)}) %reduce-scatter.5.cloned.1.call-update) | async-done | bytes 262160 | tf_op jit(solution)/shard_map/reduce_scatter | solution.py:82
  308.9 1.3 fusion.219
  310.4 1.3 fusion.112
  312.0 0.2 fusion.59
  312.7 0.9 copy.22
  313.6 149.2 %all-reduce.57.cloned.1.call-done = (f32[32,27,512]{2,0,1:T(8,128)}, f32[32,27,512]{2,0,1:T(8,128)}) async-done(((f32[32,27,512]{2,0,1:T(8,128)}, f32[32,27,512]{2,0,1:T(8,128)}), (f32[32,27,512]{2,0,1:T(8,128)}, f32[32,27,512]{2,0,1:T(8,128)})) %all-reduce.57.cloned.1.call-update) | async-done | bytes 3538960 | tf_op jit(solution)/shard_map/psum | solution.py:84
  462.8 3.1 copy.131
  465.9 1.2 copy.132
  (127 shorter events, 8.8 us)
Async XLA Ops:
  7.2 62.2 %copy-start = (bf16[32,27,512]{2,0,1:T(8,128)(2,1)S(1)}, bf16[32,27,512]{2,0,1:T(8,128)(2,1)}, u32[]{:S(2)}) copy-start(bf16[32,27,512]{2,0,1:T(8,128)(2,1)} %param.5) | copy-start | bytes 2654212
  7.2 7.7 %copy-start.4 = (bf16[1,32,4,4,128]{4,3,2,1,0:T(4,128)(2,1)S(1)}, bf16[1,32,4,4,128]{4,3,2,1,0:T(4,128)(2,1)}, u32[]{:S(2)}) copy-start(bf16[1,32,4,4,128]{4,3,2,1,0:T(4,128)(2,1)} %param.7) | copy-start | bytes 393220
  7.2 62.1 %all-gather.3.cloned.1.call-start = ((), (), s32[]{:S(2)}) async-start(), calls=%async_computation.2 | async-start | bytes 2228224 | tf_op jit(solution)/shard_map/all_gather | solution.py:60
  12.0 148.7 %reduce-scatter.3.cloned.1.call-start = ((), (), s32[]{:S(2)}) async-start(), calls=%async_computation.4 | async-start | bytes 4456448 | tf_op jit(solution)/shard_map/reduce_scatter | solution.py:73
  13.0 2.4 copy-start.7
  15.3 2.5 copy-start.5
  20.0 197.7 %all-gather.5.cloned.1.call-start = ((), (), s32[]{:S(2)}) async-start(), calls=%async_computation.3 | async-start | bytes 2228224 | tf_op jit(solution)/shard_map/all_gather | solution.py:64
  164.0 144.9 %reduce-scatter.5.cloned.1.call-start = ((), (), s32[]{:S(2)}) async-start(), calls=%async_computation.5 | async-start | bytes 4456448 | tf_op jit(solution)/shard_map/reduce_scatter | solution.py:82
  166.6 2.5 copy-start.6
  171.3 291.5 %all-reduce.57.cloned.1.call-start = ((), (), s32[]{:S(2)}) async-start(), calls=%async_computation.6 | async-start | bytes 7077888 | tf_op jit(solution)/shard_map/psum | solution.py:84
  227.4 1.0 copy-start.2
  462.8 3.1 copy-start.3
  462.8 4.3 copy-start.1
Sparse Core Ops, SparseCore 0:
  12.1 57.1 all-gather.2
  73.7 86.9 reduce-scatter.2
  164.2 53.5 all-gather.4
  221.9 86.9 reduce-scatter.4
  312.0 150.6 all-reduce.56
where the time goes:
time: 474 us
  waiting for transfers between devices  402 us (85%)
  matrix products  23.8 us (5%)
  local copies, waits for them, and re-layouts  20.3 us (4%)
  between operations  14.2 us (3%)
  other arithmetic  12.5 us (3%)
    psum x1, waiting for transfers between devices, shards(): one_grad, two_grad = lax.psum((one_grad, two_grad), 'clip')  149 us
    reduce_scatter x1, waiting for transfers between devices, shards(): lax.psum_scatter(partial_two, 'chan', scatter_dimension=0, tiled=True)  84.6 us
    reduce_scatter x1, waiting for transfers between devices, shards(): lax.psum_scatter(partial_one, 'chan', scatter_dimension=0, tiled=True)  78.7 us
    all_gather x1, waiting for transfers between devices, shards(): act_one = lax.all_gather(act_one_local, 'chan', axis=0, tiled=True)  49.3 us
    all_gather x1, waiting for transfers between devices, shards(): act_two = lax.all_gather(act_two_local, 'chan', axis=0, tiled=True)  40.5 us
    unnamed x73, local copies, waits for them, and re-layouts  11.2 us
  transfers between devices with their start and end apart: 5, of which 5 were waited for; matrix products, arithmetic and copies ran while one was open for 9% of the time, Pallas kernels for 0%

commit v1 on v0

--- a/solution.py
+++ b/solution.py
@@ -57,7 +57,9 @@
     cotangent = out_cotangent[0]
     first_float, first_pull = jax.vjp(norm_act, in_float)
     act_one_local = first_float.astype(jnp.bfloat16)
-    act_one = lax.all_gather(act_one_local, "chan", axis=0, tiled=True)
+    act_one = jnp.concatenate(
+        lax.all_to_all(jnp.stack([act_one_local] * lax.axis_size("chan")), "chan", 0, 0), axis=0
+    )
     hidden = conv_gathered(act_one, conv_one)
     second_float, second_pull = jax.vjp(norm_act, hidden)
     act_two_local = second_float.astype(jnp.bfloat16)

time: 474 us -> 421 us (0.89)
  waiting for transfers between devices: 402 us -> 318 us
  blocking collectives: 0 us -> 34.1 us
    all_gather x1 -> x0, waiting for transfers between devices: 49.3 us -> none  [shards(): act_one = lax.all_gather(act_one_local, 'chan', axis=0, tiled=True)]
    reduce_scatter x1, waiting for transfers between devices: 84.6 us -> 48.9 us  [shards(): lax.psum_scatter(partial_two, 'chan', scatter_dimension=0, tiled=True)]
    all_to_all x0 -> x1, blocking collectives: none -> 34.1 us  [shards(): lax.all_to_all(jnp.stack([act_one_local] * lax.axis_size('chan')), 'chan'...]
    unnamed x73 -> x79, local copies, waits for them, and re-layouts: 11.2 us -> 13.8 us
  transfers between devices with their start and end apart: 5 -> 4, of which waited for: 5 -> 4; matrix products, arithmetic and copies ran while one was open for 9% -> 8% of each run, Pallas kernels for 0% -> 0%
where the time goes in v1:
time: 421 us
  waiting for transfers between devices  318 us (76%)
  blocking collectives  34.1 us (8%)
  local copies, waits for them, and re-layouts  23.8 us (6%)
  matrix products  20 us (5%)
  between operations  14.2 us (3%)
  other arithmetic  10.6 us (3%)
    psum x1, waiting for transfers between devices, shards(): one_grad, two_grad = lax.psum((one_grad, two_grad), 'clip')  149 us
    reduce_scatter x1, waiting for transfers between devices, shards(): lax.psum_scatter(partial_one, 'chan', scatter_dimension=0, tiled=True)  78.7 us
    reduce_scatter x1, waiting for transfers between devices, shards(): lax.psum_scatter(partial_two, 'chan', scatter_dimension=0, tiled=True)  48.9 us
    all_gather x1, waiting for transfers between devices, shards(): act_two = lax.all_gather(act_two_local, 'chan', axis=0, tiled=True)  41.1 us
    all_to_all x1, blocking collectives, shards(): lax.all_to_all(jnp.stack([act_one_local] * lax.axis_size('chan')), 'chan'...  34.1 us
    unnamed x79, local copies, waits for them, and re-layouts  13.8 us
  transfers between devices with their start and end apart: 4, of which 4 were waited for; matrix products, arithmetic and copies ran while one was open for 8% of the time, Pallas kernels for 0%

profile of v1, /device:TPU:2, one launch (start us, length us, event | category | flops | bytes accessed | tf_op | source)
XLA Modules:
  0.0 421.1 jit_solution(7555188195193376660)
XLA Ops:
  7.2 1.0 copy.168
  10.6 2.4 fusion.4
  13.1 2.2 copy.167
  15.4 0.8 copy-done.2
  17.5 0.5 stack.188
  18.0 34.1 %all_to_all.5 = bf16[16,32,4,4,128]{4,1,3,2,0:T(8,128)(2,1)S(1)} all-to-all(bf16[16,32,4,4,128]{4,1,3,2,0:T(8,128)(2,1)S(1)} %stack.188), channel_id=1, replica_groups=mesh['clip'=16,'chan'=16] {'chan'}, dimensions={0} | all-to-all | bytes 4194304 | tf_op jit(solution)/shard_map/all_to_all | solution.py:61
  52.1 0.5 copy.49
  52.6 2.0 convolution_bitcast_fusion.1
  54.8 0.8 slice_bitcast_fusion.53
  55.7 0.9 fusion.217
  57.6 48.9 %reduce-scatter.3.cloned.1.call-done = f32[32,4,4,128]{3,0,2,1:T(8,128)} async-done(((f32[512,4,4,128]{3,0,2,1:T(8,128)}), f32[32,4,4,128]{3,0,2,1:T(8,128)}) %reduce-scatter.3.cloned.1.call-update) | async-done | bytes 262160 | tf_op jit(solution)/shard_map/reduce_scatter | solution.py:75
  106.5 2.0 multiply_reduce_fusion.3
  109.6 1.8 add_convert_fusion
  111.5 0.2 reduce-scatter.5.cloned.1.call-start
  114.0 2.4 fusion.7
  116.5 2.2 copy.166
  118.7 5.2 %convolution_bitcast_fusion.2 = f32[32,27,512]{2,0,1:T(8,128)} fusion(bf16[27,32,4,4,128]{4,1,3,2,0:T(8,128)(2,1)} %copy-done.7, bf16[512,4,4,128,1]{3,0,2,1,4:T(8,128)(2,1)S(1)} %bitcast.535), kind=kOutput, calls=%fused_computation.66 | convolution fusion | flops 1811939328 | bytes 7405568 | tf_op jit(solution)/shard_map/cthw,kothw->okc/dot_general | solution.py:78
  124.0 41.1 %all-gather.2.cloned.1.call-done = bf16[512,4,4,128]{3,0,2,1:T(8,128)(2,1)} async-done(((bf16[32,4,4,128]{3,0,2,1:T(8,128)(2,1)}), bf16[512,4,4,128]{3,0,2,1:T(8,128)(2,1)}) %all-gather.2.cloned.1.call-update) | async-done | bytes 2097168 | tf_op jit(solution)/shard_map/all_gather | solution.py:66
  165.1 5.9 %fusion.13 = f32[32,27,512]{2,0,1:T(8,128)} fusion(bf16[27,32,4,4,128]{4,1,3,2,0:T(8,128)(2,1)} %copy-done.6, bf16[512,4,4,128]{3,0,2,1:T(8,128)(2,1)} %all-gather.2.cloned.1.call-done), kind=kOutput, calls=%fused_computation.65 | convolution fusion | flops 1811939328 | bytes 7405568 | tf_op jit(solution)/shard_map/cthw,kothw->okc/dot_general | solution.py:69
  171.0 1.6 copy-done.8
  172.8 2.0 convolution_bitcast_fusion
  175.0 1.0 slice_bitcast_fusion.26
  176.0 0.8 fusion.43
  176.9 0.9 copy.87
  177.7 78.7 %reduce-scatter.5.cloned.1.call-done = f32[32,4,4,128]{3,0,2,1:T(8,128)} async-done(((f32[512,4,4,128]{3,0,2,1:T(8,128)}), f32[32,4,4,128]{3,0,2,1:T(8,128)}) %reduce-scatter.5.cloned.1.call-update) | async-done | bytes 262160 | tf_op jit(solution)/shard_map/reduce_scatter | solution.py:84
  256.5 1.3 fusion.214
  257.9 1.3 fusion.106
  259.6 0.2 fusion.53
  260.3 0.9 copy.88
  261.2 149.1 %all-reduce.57.cloned.1.call-done = (f32[32,27,512]{2,0,1:T(8,128)}, f32[32,27,512]{2,0,1:T(8,128)}) async-done(((f32[32,27,512]{2,0,1:T(8,128)}, f32[32,27,512]{2,0,1:T(8,128)}), (f32[32,27,512]{2,0,1:T(8,128)}, f32[32,27,512]{2,0,1:T(8,128)})) %all-reduce.57.cloned.1.call-update) | async-done | bytes 3538960 | tf_op jit(solution)/shard_map/psum | solution.py:86
  410.3 3.1 copy.223
  413.4 1.2 copy.224
  (133 shorter events, 9.7 us)
Async XLA Ops:
  7.2 45.4 %copy-start = (bf16[32,27,512]{2,0,1:T(8,128)(2,1)S(1)}, bf16[32,27,512]{2,0,1:T(8,128)(2,1)}, u32[]{:S(2)}) copy-start(bf16[32,27,512]{2,0,1:T(8,128)(2,1)} %param.5) | copy-start | bytes 2654212
  7.2 3.0 copy-start.4
  7.2 99.3 %reduce-scatter.3.cloned.1.call-start = ((), (), s32[]{:S(2)}) async-start(), calls=%async_computation.4 | async-start | bytes 4456448 | tf_op jit(solution)/shard_map/reduce_scatter | solution.py:75
  8.3 2.4 copy-start.9
  10.6 2.5 copy-start.6
  15.3 0.9 copy-start.2
  15.3 149.8 %all-gather.2.cloned.1.call-start = ((), (), s32[]{:S(2)}) async-start(), calls=%async_computation.3 | async-start | bytes 2228224 | tf_op jit(solution)/shard_map/all_gather | solution.py:66
  111.5 145.0 %reduce-scatter.5.cloned.1.call-start = ((), (), s32[]{:S(2)}) async-start(), calls=%async_computation.5 | async-start | bytes 4456448 | tf_op jit(solution)/shard_map/reduce_scatter | solution.py:84
  114.0 2.5 copy-start.7
  118.7 291.6 %all-reduce.57.cloned.1.call-start = ((), (), s32[]{:S(2)}) async-start(), calls=%async_computation.6 | async-start | bytes 7077888 | tf_op jit(solution)/shard_map/psum | solution.py:86
  171.0 1.6 copy-start.8
  171.0 1.8 copy-start.10
  176.0 84.1 %copy-start.5 = (bf16[1,32,4,4,128]{4,3,2,1,0:T(4,128)(2,1)S(1)}, bf16[1,32,4,4,128]{4,3,2,1,0:T(4,128)(2,1)}, u32[]{:S(2)}) copy-start(bf16[1,32,4,4,128]{4,3,2,1,0:T(4,128)(2,1)} %param.7) | copy-start | bytes 393220
  410.3 3.1 copy-start.3
  410.3 4.3 %copy-start.1 = (bf16[32,27,512]{2,0,1:T(8,128)(2,1)S(1)}, bf16[32,27,512]{2,0,1:T(8,128)(2,1)}, u32[]{:S(2)}) copy-start(bf16[32,27,512]{2,0,1:T(8,128)(2,1)} %param.5) | copy-start | bytes 2654212
Sparse Core Ops, SparseCore 0:
  15.5 90.9 reduce-scatter.2
  111.6 53.4 all-gather.1
  169.5 86.9 reduce-scatter.4
  259.6 150.6 all-reduce.56
